TPU v7x, 256 devices: a whole 4x4x8 slice. The times are simulated.
256 devices in a mesh: band: 32 (over y, z), chan: 8 (over x, core).
Axes of the slice: x: 4, y: 4, z: 8, core: 2. Of those that a mesh axis runs over, the one named last changes fastest.
Arguments:
- new_frames: bfloat16 [4, 128, 512, 320], P(None, 'band', 'chan'), may hold values from -6 to 6
- cached_frames: bfloat16 [2, 128, 512, 320], P(None, 'band', 'chan'), may hold values from -6 to 6
- conv_weight: bfloat16 [3, 3, 3, 512, 512], P(None, None, None, 'chan'), may hold values from -0.0546875 to 0.0546875
- out_bias: float32 [512], P('chan'), may hold values from -3 to 3
Outputs:
- conv_out: bfloat16 [4, 128, 512, 320], P(None, 'band', 'chan')
All inputs are finite; a program needn't handle non-finite values.
Results may differ from a plain program's by a relative error of at most 0.001.
Values may be sent and summed in bfloat16 or wider, within the bound.
No kernel may reach another device: no remote copies, remote signals or barrier semaphores. Data moves between devices by JAX's collectives and lax.ppermute only.
A program may use at most 128 MiB of HBM per device.

v0:
```python
import jax
import jax.numpy as jnp
from jax import lax
from jax.sharding import PartitionSpec as P


def with_halo(block, sides, width):
    for axis, dim in sides:
        count = lax.axis_size(axis)
        forward = [(i, i + 1) for i in range(count - 1)]
        backward = [(target, source) for source, target in forward]
        low = lax.ppermute(
            lax.slice_in_dim(block, block.shape[dim] - width, None, axis=dim), axis, forward
        )
        high = lax.ppermute(lax.slice_in_dim(block, 0, width, axis=dim), axis, backward)
        block = jnp.concatenate([low, block, high], axis=dim)
    return block


def convolve(padded, kernel):
    frame_count = padded.shape[0] - 2
    row_count = padded.shape[1] - 2
    col_count = padded.shape[3] - 2
    summed = jnp.zeros((frame_count, row_count, kernel.shape[3], col_count), jnp.float32)
    for time_tap in range(3):
        for row_tap in range(3):
            window = padded[time_tap : time_tap + frame_count, row_tap : row_tap + row_count]
            products = jnp.einsum(
                "kdc,frcw->kfrdw",
                kernel[time_tap, row_tap],
                window,
                preferred_element_type=jnp.float32,
            )
            summed = (
                summed
                + products[0, :, :, :, 0:col_count]
                + products[1, :, :, :, 1 : col_count + 1]
                + products[2, :, :, :, 2 : col_count + 2]
            )
    return summed


def pad_columns(layered):
    return jnp.pad(layered, ((0, 0), (0, 0), (0, 0), (1, 1)))


def on_device(new_frames, cached_frames, conv_weight, out_bias):
    stacked = jnp.concatenate([cached_frames, new_frames], axis=0)
    rimmed = with_halo(stacked, (("band", 1),), 1)
    summed = convolve(pad_columns(lax.all_gather(rimmed, "chan", axis=2, tiled=True)), conv_weight)
    return (summed + out_bias[None, None, :, None]).astype(jnp.bfloat16)


def solution(mesh):
    in_specs = (
        P(None, "band", "chan", None),
        P(None, "band", "chan", None),
        P(None, None, None, "chan", None),
        P("chan"),
    )
    out_specs = P(None, "band", "chan", None)
    return jax.shard_map(
        on_device, mesh=mesh, in_specs=in_specs, out_specs=out_specs, check_vma=False
    )
```

profile of v0, /device:TPU:1, one launch (start us, length us, event | category | flops | bytes accessed | tf_op | source)
XLA Modules:
  0.0 180.6 jit_solution(579651613324927364)
XLA Ops:
  6.5 0.0 all-gather.2.cloned.1.call-start
  6.5 1.0 constant_dynamic-update-slice_fusion.1
  7.6 1.3 constant_dynamic-update-slice_fusion
  8.9 0.1 fusion.105
  8.9 4.4 %collective-permute-start = (bf16[6,1,64,320]{3,2,1,0:T(8,128)(2,1)S(1)}, bf16[6,1,64,320]{3,2,1,0:T(8,128)(2,1)S(1)}, u32[]{:S(2)}, u32[]{:S(2)}) collective-permute-start(bf16[6,1,64,320]{3,2,1,0:T(8,128)(2,1)S(1)} %get-tuple-element.5), channel_id=1, source_target_pairs={{0,8},{8,16},{16,24},{24,32},{32,40},{40,48},{48,56},{56,64},{64,7... | collective-permute-start | bytes 737288 | tf_op jit(solution)/shard_map/ppermute | solution.py:12
  13.3 1.3 collective-permute-start.1
  14.6 4.4 %collective-permute-done = bf16[6,1,64,320]{3,2,1,0:T(8,128)(2,1)S(1)} collective-permute-done((bf16[6,1,64,320]{3,2,1,0:T(8,128)(2,1)S(1)}, bf16[6,1,64,320]{3,2,1,0:T(8,128)(2,1)S(1)}, u32[]{:S(2)}, u32[]{:S(2)}) %collective-permute-start) | collective-permute-done | bytes 245792 | tf_op jit(solution)/shard_map/ppermute | solution.py:12
  19.0 4.2 %collective-permute-done.1 = bf16[6,1,64,320]{3,2,1,0:T(8,128)(2,1)S(1)} collective-permute-done((bf16[6,1,64,320]{3,2,1,0:T(8,128)(2,1)S(1)}, bf16[6,1,64,320]{3,2,1,0:T(8,128)(2,1)S(1)}, u32[]{:S(2)}, u32[]{:S(2)}) %collective-permute-start.1) | collective-permute-done | bytes 245792 | tf_op jit(solution)/shard_map/ppermute | solution.py:15
  23.2 1.6 pad_maximum_fusion
  24.8 0.0 all-gather.2.cloned.1.call-update
  24.8 0.0 copy-start.1
  24.8 80.6 %all-gather.2.cloned.1.call-done = bf16[6,6,512,320]{3,2,1,0:T(8,128)(2,1)} async-done(((bf16[6,6,64,320]{3,2,1,0:T(8,128)(2,1)}), bf16[6,6,512,320]{3,2,1,0:T(8,128)(2,1)}) %all-gather.2.cloned.1.call-update) | async-done | bytes 11796496 | tf_op jit(solution)/shard_map/all_gather | solution.py:50
  105.4 16.7 %copy.13 = bf16[6,6,512,320]{2,3,1,0:T(8,128)(2,1)} copy(bf16[6,6,512,320]{3,2,1,0:T(8,128)(2,1)} %all-gather.2.cloned.1.call-done) | data formatting | bytes 23592960 | tf_op jit(solution)/shard_map/all_gather | solution.py:50
  122.1 0.0 copy-done.1
  122.1 0.0 copy-start
  122.1 4.5 %fusion.42 = f32[3,4,4,64,322]{4,3,0,2,1:T(8,128)S(1)} fusion(bf16[6,6,512,320]{2,3,1,0:T(8,128)(2,1)} %copy.13, bf16[3,3,3,64,512]{4,3,2,1,0:T(8,128)(2,1)S(1)} %copy-done.1), kind=kOutput, calls=%fused_computation.32 | convolution fusion | flops 1012924416 | bytes 15949824 | tf_op jit(solution)/shard_map/kdc,frcw->kfrdw/dot_general | solution.py:28
  126.6 1.4 copy-done
  128.0 1.9 %fusion.45 = f32[3,4,4,64,322]{4,3,0,2,1:T(8,128)S(1)} fusion(bf16[6,6,512,320]{2,3,1,0:T(8,128)(2,1)S(1)} %copy-done, bf16[3,3,3,64,512]{4,3,2,1,0:T(8,128)(2,1)S(1)} %copy-done.1), kind=kOutput, calls=%fused_computation.33 | convolution fusion | flops 1012924416 | bytes 15949824 | tf_op jit(solution)/shard_map/kdc,frcw->kfrdw/dot_general | solution.py:28
  129.9 4.1 %fusion.48 = f32[3,4,4,64,322]{4,3,0,2,1:T(8,128)} fusion(bf16[6,6,512,320]{2,3,1,0:T(8,128)(2,1)S(1)} %copy-done, bf16[3,3,3,64,512]{4,3,2,1,0:T(8,128)(2,1)S(1)} %copy-done.1), kind=kOutput, calls=%fused_computation.34 | convolution fusion | flops 1012924416 | bytes 15949824 | tf_op jit(solution)/shard_map/kdc,frcw->kfrdw/dot_general | solution.py:28
  134.0 4.1 %fusion.51 = f32[3,4,4,64,322]{4,3,0,2,1:T(8,128)} fusion(bf16[6,6,512,320]{2,3,1,0:T(8,128)(2,1)S(1)} %copy-done, bf16[3,3,3,64,512]{4,3,2,1,0:T(8,128)(2,1)S(1)} %copy-done.1), kind=kOutput, calls=%fused_computation.35 | convolution fusion | flops 1012924416 | bytes 15949824 | tf_op jit(solution)/shard_map/kdc,frcw->kfrdw/dot_general | solution.py:28
  138.1 4.0 %fusion.27 = f32[3,4,4,64,322]{4,3,2,1,0:T(8,128)} fusion(bf16[6,6,512,320]{2,3,1,0:T(8,128)(2,1)S(1)} %copy-done, bf16[3,3,3,64,512]{4,3,2,1,0:T(8,128)(2,1)S(1)} %copy-done.1), kind=kOutput, calls=%fused_computation.27 | convolution fusion | flops 1012924416 | bytes 15949824 | tf_op jit(solution)/shard_map/kdc,frcw->kfrdw/dot_general | solution.py:28
  142.1 4.1 %fusion.30 = f32[3,4,4,64,322]{4,3,2,1,0:T(8,128)} fusion(bf16[6,6,512,320]{2,3,1,0:T(8,128)(2,1)S(1)} %copy-done, bf16[3,3,3,64,512]{4,3,2,1,0:T(8,128)(2,1)S(1)} %copy-done.1), kind=kOutput, calls=%fused_computation.28 | convolution fusion | flops 1012924416 | bytes 15949824 | tf_op jit(solution)/shard_map/kdc,frcw->kfrdw/dot_general | solution.py:28
  146.3 4.1 %fusion.33 = f32[3,4,4,64,322]{4,3,2,1,0:T(8,128)} fusion(bf16[6,6,512,320]{2,3,1,0:T(8,128)(2,1)S(1)} %copy-done, bf16[3,3,3,64,512]{4,3,2,1,0:T(8,128)(2,1)S(1)} %copy-done.1), kind=kOutput, calls=%fused_computation.29 | convolution fusion | flops 1012924416 | bytes 15949824 | tf_op jit(solution)/shard_map/kdc,frcw->kfrdw/dot_general | solution.py:28
  150.3 4.2 %fusion.36 = f32[3,4,4,64,322]{4,3,2,1,0:T(8,128)} fusion(bf16[6,6,512,320]{2,3,1,0:T(8,128)(2,1)S(1)} %copy-done, bf16[3,3,3,64,512]{4,3,2,1,0:T(8,128)(2,1)S(1)} %copy-done.1), kind=kOutput, calls=%fused_computation.30 | convolution fusion | flops 1012924416 | bytes 15949824 | tf_op jit(solution)/shard_map/kdc,frcw->kfrdw/dot_general | solution.py:28
  154.6 0.0 copy-start.2
  154.6 4.0 %fusion.39 = f32[3,4,4,64,322]{4,3,0,2,1:T(8,128)} fusion(bf16[6,6,512,320]{2,3,1,0:T(8,128)(2,1)S(1)} %copy-done, bf16[3,3,3,64,512]{4,3,2,1,0:T(8,128)(2,1)S(1)} %copy-done.1), kind=kOutput, calls=%fused_computation.31 | convolution fusion | flops 1012924416 | bytes 15949824 | tf_op jit(solution)/shard_map/kdc,frcw->kfrdw/dot_general | solution.py:28
  158.6 0.0 copy-done.2
  158.6 15.1 %fusion.65 = bf16[4,4,64,320]{3,2,1,0:T(8,128)(2,1)} fusion(f32[3,4,4,64,322]{4,3,2,1,0:T(8,128)} %fusion.36, f32[3,4,4,64,322]{4,3,2,1,0:T(8,128)} %fusion.33, f32[3,4,4,64,322]{4,3,2,1,0:T(8,128)} %fusion.30, f32[3,4,4,64,322]{4,3,2,1,0:T(8,128)} %fusion.27, f32[3,4,4,64,322]{4,3,0,2,1:T(8,128)} %fusion.51, f32[3,4,4,64,322]{4,3,0,2,1:T(8,128)} %fusion.48, ...), kind=kLoop, calls=%fused_computation.49 | loop fusion | flops 9175040 | bytes 36045056 | tf_op jit(solution)/shard_map/convert_element_type | solution.py:51
Async XLA Ops:
  6.5 98.8 %all-gather.2.cloned.1.call-start = ((), (), s32[]{:S(2)}) async-start(), calls=%async_computation | async-start | bytes 15925248 | tf_op jit(solution)/shard_map/all_gather | solution.py:50
  8.9 10.0 %collective-permute-start = (bf16[6,1,64,320]{3,2,1,0:T(8,128)(2,1)S(1)}, bf16[6,1,64,320]{3,2,1,0:T(8,128)(2,1)S(1)}, u32[]{:S(2)}, u32[]{:S(2)}) collective-permute-start(bf16[6,1,64,320]{3,2,1,0:T(8,128)(2,1)S(1)} %get-tuple-element.5), channel_id=1, source_target_pairs={{0,8},{8,16},{16,24},{24,32},{32,40},{40,48},{48,56},{56,64},{64,7... | collective-permute-start | bytes 737288 | tf_op jit(solution)/shard_map/ppermute | solution.py:12
  13.3 9.8 %collective-permute-start.1 = (bf16[6,1,64,320]{3,2,1,0:T(8,128)(2,1)S(1)}, bf16[6,1,64,320]{3,2,1,0:T(8,128)(2,1)S(1)}, u32[]{:S(2)}, u32[]{:S(2)}) collective-permute-start(bf16[6,1,64,320]{3,2,1,0:T(8,128)(2,1)S(1)} %get-tuple-element.6), channel_id=1, source_target_pairs={{8,0},{16,8},{24,16},{32,24},{40,32},{48,40},{56,48},{64,56},{72,6... | collective-permute-start | bytes 737288 | tf_op jit(solution)/shard_map/ppermute | solution.py:15
  24.8 97.3 %copy-start.1 = (bf16[3,3,3,64,512]{4,3,2,1,0:T(8,128)(2,1)S(1)}, bf16[3,3,3,64,512]{4,3,2,1,0:T(8,128)(2,1)}, u32[]{:S(2)}) copy-start(bf16[3,3,3,64,512]{4,3,2,1,0:T(8,128)(2,1)} %param.6) | copy-start | bytes 5308420
  122.1 5.9 %copy-start = (bf16[6,6,512,320]{2,3,1,0:T(8,128)(2,1)S(1)}, bf16[6,6,512,320]{2,3,1,0:T(8,128)(2,1)}, u32[]{:S(2)}) copy-start(bf16[6,6,512,320]{2,3,1,0:T(8,128)(2,1)} %copy.13) | copy-start | bytes 35389444
  154.6 4.0 %copy-start.2 = (f32[64]{0:T(128)S(1)}, f32[64]{0:T(128)}, u32[]{:S(2)}) copy-start(f32[64]{0:T(128)} %param.7) | copy-start | bytes 772
Sparse Core Ops, SparseCore 0:
  24.9 80.4 all-gather.1
where the time goes:
time: 181 us
  waiting for transfers between devices  89.1 us (49%)
  matrix products  35.1 us (19%)
  local copies, waits for them, and re-layouts  20.5 us (11%)
  other arithmetic  16.7 us (9%)
  between operations  13.5 us (7%)
  starting transfers between devices  5.67 us (3%)
    all_gather x1, waiting for transfers between devices, on_device(): lax.all_gather(rimmed, 'chan', axis=2, tiled=True)  80.6 us
    dot_general x9, matrix products, convolve(): jnp.einsum('kdc,frcw->kfrdw', kernel[time_tap, row_tap], window, preferre...  35.1 us
    all_gather x1, local copies, waits for them, and re-layouts, on_device(): lax.all_gather(rimmed, 'chan', axis=2, tiled=True)  16.7 us
    convert_element_type x1, other arithmetic, on_device(): return (summed + out_bias[None, None, :, None]).astype(jnp.bfloat16)  15.1 us
    ppermute x1, starting transfers between devices, with_halo(): lax.ppermute(lax.slice_in_dim(block, block.shape[dim] - width, None, axis...  4.38 us
    ppermute x1, waiting for transfers between devices, with_halo(): lax.ppermute(lax.slice_in_dim(block, block.shape[dim] - width, None, axis...  4.36 us
    ppermute x1, waiting for transfers between devices, with_halo(): lax.ppermute(lax.slice_in_dim(block, 0, width, axis=dim), axis, backward)  4.19 us
  transfers between devices with their start and end apart: 3, of which 3 were waited for; matrix products, arithmetic and copies ran while one was open for 0% of the time, Pallas kernels for 0%

commit v1 on v0

--- a/solution.py
+++ b/solution.py
@@ -2,6 +2,11 @@
 import jax.numpy as jnp
 from jax import lax
 from jax.sharding import PartitionSpec as P
+
+
+def all_by_exchange(x, mesh_axis, dim):
+    repeated = jnp.stack([x] * lax.axis_size(mesh_axis))
+    return jnp.concatenate(lax.all_to_all(repeated, mesh_axis, 0, 0), axis=dim)
 
 
 def with_halo(block, sides, width):
@@ -47,7 +52,7 @@
 def on_device(new_frames, cached_frames, conv_weight, out_bias):
     stacked = jnp.concatenate([cached_frames, new_frames], axis=0)
     rimmed = with_halo(stacked, (("band", 1),), 1)
-    summed = convolve(pad_columns(lax.all_gather(rimmed, "chan", axis=2, tiled=True)), conv_weight)
+    summed = convolve(pad_columns(all_by_exchange(rimmed, "chan", 2)), conv_weight)
     return (summed + out_bias[None, None, :, None]).astype(jnp.bfloat16)
 
 

time: 181 us -> 258 us (1.43); the launches traced: 181 us -> 255 us
  blocking collectives: 0 us -> 161 us
  waiting for transfers between devices: 89.1 us -> 8.55 us
  between operations: 13.5 us -> 0.23 us
  local copies, waits for them, and re-layouts: 20.5 us -> 28.8 us
    all_to_all x0 -> x1, blocking collectives: none -> 161 us  [all_by_exchange(): return jnp.concatenate(lax.all_to_all(repeated, mesh_axis, 0, 0), axis=dim)]
    all_gather x1 -> x0, waiting for transfers between devices: 80.6 us -> none  [on_device(): lax.all_gather(rimmed, 'chan', axis=2, tiled=True)]
    reshape x0 -> x2, local copies, waits for them, and re-layouts: none -> 22.8 us  [all_by_exchange(): return jnp.concatenate(lax.all_to_all(repeated, mesh_axis, 0, 0), axis=dim)]
    all_gather x1 -> x0, local copies, waits for them, and re-layouts: 16.7 us -> none  [on_device(): lax.all_gather(rimmed, 'chan', axis=2, tiled=True)]
  transfers between devices with their start and end apart: 3 -> 2, of which waited for: 3 -> 2; matrix products, arithmetic and copies ran while one was open for 0% -> 0% of each run, Pallas kernels for 0% -> 0%
where the time goes in v1:
time: 258 us; the launch traced here: 255 us
  blocking collectives  161 us (62%)
  matrix products  35.1 us (14%)
  local copies, waits for them, and re-layouts  28.8 us (11%)
  other arithmetic  15.5 us (6%)
  waiting for transfers between devices  8.55 us (3%)
  starting transfers between devices  5.67 us (2%)
    all_to_all x1, blocking collectives, all_by_exchange(): return jnp.concatenate(lax.all_to_all(repeated, mesh_axis, 0, 0), axis=dim)  161 us
    dot_general x9, matrix products, convolve(): jnp.einsum('kdc,frcw->kfrdw', kernel[time_tap, row_tap], window, preferre...  35.1 us
    reshape x2, local copies, waits for them, and re-layouts, all_by_exchange(): return jnp.concatenate(lax.all_to_all(repeated, mesh_axis, 0, 0), axis=dim)  22.8 us
    convert_element_type x1, other arithmetic, on_device(): return (summed + out_bias[None, None, :, None]).astype(jnp.bfloat16)  15.1 us
  transfers between devices with their start and end apart: 2, of which 2 were waited for; matrix products, arithmetic and copies ran while one was open for 0% of the time, Pallas kernels for 0%

profile of v1, /device:TPU:1, one launch (start us, length us, event | category | flops | bytes accessed | tf_op | source)
XLA Modules:
  0.0 254.9 jit_solution(9692253513439810647)
XLA Ops:
  0.0 1.0 constant_dynamic-update-slice_fusion.1
  1.0 1.3 constant_dynamic-update-slice_fusion
  2.3 0.1 fusion.105
  2.4 4.4 %collective-permute-start = (bf16[6,1,64,320]{3,2,1,0:T(8,128)(2,1)S(1)}, bf16[6,1,64,320]{3,2,1,0:T(8,128)(2,1)S(1)}, u32[]{:S(2)}, u32[]{:S(2)}) collective-permute-start(bf16[6,1,64,320]{3,2,1,0:T(8,128)(2,1)S(1)} %get-tuple-element.5), channel_id=1, source_target_pairs={{0,8},{8,16},{16,24},{24,32},{32,40},{40,48},{48,56},{56,64},{64,7... | collective-permute-start | bytes 737288 | tf_op jit(solution)/shard_map/ppermute | solution.py:17
  6.8 1.3 collective-permute-start.1
  8.1 4.4 %collective-permute-done = bf16[6,1,64,320]{3,2,1,0:T(8,128)(2,1)S(1)} collective-permute-done((bf16[6,1,64,320]{3,2,1,0:T(8,128)(2,1)S(1)}, bf16[6,1,64,320]{3,2,1,0:T(8,128)(2,1)S(1)}, u32[]{:S(2)}, u32[]{:S(2)}) %collective-permute-start) | collective-permute-done | bytes 245792 | tf_op jit(solution)/shard_map/ppermute | solution.py:17
  12.5 4.2 %collective-permute-done.1 = bf16[6,1,64,320]{3,2,1,0:T(8,128)(2,1)S(1)} collective-permute-done((bf16[6,1,64,320]{3,2,1,0:T(8,128)(2,1)S(1)}, bf16[6,1,64,320]{3,2,1,0:T(8,128)(2,1)S(1)}, u32[]{:S(2)}, u32[]{:S(2)}) %collective-permute-start.1) | collective-permute-done | bytes 245792 | tf_op jit(solution)/shard_map/ppermute | solution.py:20
  16.6 0.4 pad_maximum_fusion
  17.0 2.3 stack.2
  19.3 161.1 %all_to_all.5 = bf16[8,6,6,64,320]{4,3,2,1,0:T(8,128)(2,1)S(1)} all-to-all(bf16[8,6,6,64,320]{4,3,2,1,0:T(8,128)(2,1)S(1)} %stack.2), channel_id=1, replica_groups=mesh['band'=32,'chan'=8] {'chan'}, dimensions={0} | all-to-all | bytes 23592960 | tf_op jit(solution)/shard_map/all_to_all | solution.py:9
  180.4 5.9 %copy.19 = bf16[6,6,8,64,320]{4,3,2,1,0:T(8,128)(2,1)} copy(bf16[6,6,8,64,320]{4,3,1,0,2:T(8,128)(2,1)S(1)} %bitcast.218) | data formatting | bytes 23592960 | tf_op jit(solution)/shard_map/reshape | solution.py:9
  186.3 0.0 copy-start.1
  186.3 16.8 %copy.20 = bf16[6,6,512,320]{2,3,1,0:T(8,128)(2,1)} copy(bf16[6,6,512,320]{3,2,1,0:T(8,128)(2,1)} %bitcast.219) | data formatting | bytes 23592960 | tf_op jit(solution)/shard_map/reshape | solution.py:9
  203.2 0.0 copy-done.1
  203.2 0.0 copy-start
  203.2 4.5 %fusion.42 = f32[3,4,4,64,322]{4,3,0,2,1:T(8,128)S(1)} fusion(bf16[6,6,512,320]{2,3,1,0:T(8,128)(2,1)} %copy.20, bf16[3,3,3,64,512]{4,3,2,1,0:T(8,128)(2,1)S(1)} %copy-done.1), kind=kOutput, calls=%fused_computation.32 | convolution fusion | flops 1012924416 | bytes 15949824 | tf_op jit(solution)/shard_map/kdc,frcw->kfrdw/dot_general | solution.py:33
  207.7 1.4 copy-done
  209.1 1.9 fusion.45
  211.0 4.1 %fusion.48 = f32[3,4,4,64,322]{4,3,0,2,1:T(8,128)} fusion(bf16[6,6,512,320]{2,3,1,0:T(8,128)(2,1)S(1)} %copy-done, bf16[3,3,3,64,512]{4,3,2,1,0:T(8,128)(2,1)S(1)} %copy-done.1), kind=kOutput, calls=%fused_computation.34 | convolution fusion | flops 1012924416 | bytes 15949824 | tf_op jit(solution)/shard_map/kdc,frcw->kfrdw/dot_general | solution.py:33
  215.1 4.1 %fusion.51 = f32[3,4,4,64,322]{4,3,0,2,1:T(8,128)} fusion(bf16[6,6,512,320]{2,3,1,0:T(8,128)(2,1)S(1)} %copy-done, bf16[3,3,3,64,512]{4,3,2,1,0:T(8,128)(2,1)S(1)} %copy-done.1), kind=kOutput, calls=%fused_computation.35 | convolution fusion | flops 1012924416 | bytes 15949824 | tf_op jit(solution)/shard_map/kdc,frcw->kfrdw/dot_general | solution.py:33
  219.2 4.0 %fusion.27 = f32[3,4,4,64,322]{4,3,2,1,0:T(8,128)} fusion(bf16[6,6,512,320]{2,3,1,0:T(8,128)(2,1)S(1)} %copy-done, bf16[3,3,3,64,512]{4,3,2,1,0:T(8,128)(2,1)S(1)} %copy-done.1), kind=kOutput, calls=%fused_computation.27 | convolution fusion | flops 1012924416 | bytes 15949824 | tf_op jit(solution)/shard_map/kdc,frcw->kfrdw/dot_general | solution.py:33
  223.2 4.1 %fusion.30 = f32[3,4,4,64,322]{4,3,2,1,0:T(8,128)} fusion(bf16[6,6,512,320]{2,3,1,0:T(8,128)(2,1)S(1)} %copy-done, bf16[3,3,3,64,512]{4,3,2,1,0:T(8,128)(2,1)S(1)} %copy-done.1), kind=kOutput, calls=%fused_computation.28 | convolution fusion | flops 1012924416 | bytes 15949824 | tf_op jit(solution)/shard_map/kdc,frcw->kfrdw/dot_general | solution.py:33
  227.3 4.1 %fusion.33 = f32[3,4,4,64,322]{4,3,2,1,0:T(8,128)} fusion(bf16[6,6,512,320]{2,3,1,0:T(8,128)(2,1)S(1)} %copy-done, bf16[3,3,3,64,512]{4,3,2,1,0:T(8,128)(2,1)S(1)} %copy-done.1), kind=kOutput, calls=%fused_computation.29 | convolution fusion | flops 1012924416 | bytes 15949824 | tf_op jit(solution)/shard_map/kdc,frcw->kfrdw/dot_general | solution.py:33
  231.4 4.2 %fusion.36 = f32[3,4,4,64,322]{4,3,2,1,0:T(8,128)} fusion(bf16[6,6,512,320]{2,3,1,0:T(8,128)(2,1)S(1)} %copy-done, bf16[3,3,3,64,512]{4,3,2,1,0:T(8,128)(2,1)S(1)} %copy-done.1), kind=kOutput, calls=%fused_computation.30 | convolution fusion | flops 1012924416 | bytes 15949824 | tf_op jit(solution)/shard_map/kdc,frcw->kfrdw/dot_general | solution.py:33
  235.6 0.0 copy-start.2
  235.6 4.0 %fusion.39 = f32[3,4,4,64,322]{4,3,0,2,1:T(8,128)} fusion(bf16[6,6,512,320]{2,3,1,0:T(8,128)(2,1)S(1)} %copy-done, bf16[3,3,3,64,512]{4,3,2,1,0:T(8,128)(2,1)S(1)} %copy-done.1), kind=kOutput, calls=%fused_computation.31 | convolution fusion | flops 1012924416 | bytes 15949824 | tf_op jit(solution)/shard_map/kdc,frcw->kfrdw/dot_general | solution.py:33
  239.7 0.0 copy-done.2
  239.7 15.1 %fusion.65 = bf16[4,4,64,320]{3,2,1,0:T(8,128)(2,1)} fusion(f32[3,4,4,64,322]{4,3,2,1,0:T(8,128)} %fusion.36, f32[3,4,4,64,322]{4,3,2,1,0:T(8,128)} %fusion.33, f32[3,4,4,64,322]{4,3,2,1,0:T(8,128)} %fusion.30, f32[3,4,4,64,322]{4,3,2,1,0:T(8,128)} %fusion.27, f32[3,4,4,64,322]{4,3,0,2,1:T(8,128)} %fusion.51, f32[3,4,4,64,322]{4,3,0,2,1:T(8,128)} %fusion.48, ...), kind=kLoop, calls=%fused_computation.49 | loop fusion | flops 9175040 | bytes 36045056 | tf_op jit(solution)/shard_map/convert_element_type | solution.py:56
Async XLA Ops:
  2.4 10.0 %collective-permute-start = (bf16[6,1,64,320]{3,2,1,0:T(8,128)(2,1)S(1)}, bf16[6,1,64,320]{3,2,1,0:T(8,128)(2,1)S(1)}, u32[]{:S(2)}, u32[]{:S(2)}) collective-permute-start(bf16[6,1,64,320]{3,2,1,0:T(8,128)(2,1)S(1)} %get-tuple-element.5), channel_id=1, source_target_pairs={{0,8},{8,16},{16,24},{24,32},{32,40},{40,48},{48,56},{56,64},{64,7... | collective-permute-start | bytes 737288 | tf_op jit(solution)/shard_map/ppermute | solution.py:17
  6.8 9.8 %collective-permute-start.1 = (bf16[6,1,64,320]{3,2,1,0:T(8,128)(2,1)S(1)}, bf16[6,1,64,320]{3,2,1,0:T(8,128)(2,1)S(1)}, u32[]{:S(2)}, u32[]{:S(2)}) collective-permute-start(bf16[6,1,64,320]{3,2,1,0:T(8,128)(2,1)S(1)} %get-tuple-element.6), channel_id=1, source_target_pairs={{8,0},{16,8},{24,16},{32,24},{40,32},{48,40},{56,48},{64,56},{72,6... | collective-permute-start | bytes 737288 | tf_op jit(solution)/shard_map/ppermute | solution.py:20
  186.3 16.8 %copy-start.1 = (bf16[3,3,3,64,512]{4,3,2,1,0:T(8,128)(2,1)S(1)}, bf16[3,3,3,64,512]{4,3,2,1,0:T(8,128)(2,1)}, u32[]{:S(2)}) copy-start(bf16[3,3,3,64,512]{4,3,2,1,0:T(8,128)(2,1)} %param.6) | copy-start | bytes 5308420
  203.2 5.9 %copy-start = (bf16[6,6,512,320]{2,3,1,0:T(8,128)(2,1)S(1)}, bf16[6,6,512,320]{2,3,1,0:T(8,128)(2,1)}, u32[]{:S(2)}) copy-start(bf16[6,6,512,320]{2,3,1,0:T(8,128)(2,1)} %copy.20) | copy-start | bytes 35389444
  235.6 4.1 %copy-start.2 = (f32[64]{0:T(128)S(1)}, f32[64]{0:T(128)}, u32[]{:S(2)}) copy-start(f32[64]{0:T(128)} %param.7) | copy-start | bytes 772
